TPU v7x, 32 devices: a whole 2x2x4 slice. The times are simulated.
32 devices in a mesh: fsdp: 4 (over y, x), ctx: 4 (over z), tp: 2 (over core).
Axes of the slice: x: 2, y: 2, z: 4, core: 2. Of those that a mesh axis runs over, the one named last changes fastest.
Arguments:
- inputs: bfloat16 [4, 1024, 2048], P('fsdp', 'ctx'), may hold values from -6 to 6
- positions: int32 [4, 1024], P('fsdp', 'ctx'), may hold values from 0 to 1535, as said below
- blocks: int32 [4, 1024], P('fsdp', 'ctx'), may hold values from 0 to 7, never falling along the last dimension, each value on 1 to 256 neighbouring positions
- cotangent: bfloat16 [4, 1024, 2048], P('fsdp', 'ctx'), may hold values from -6 to 6
- attn_gain: bfloat16 [2048], P('fsdp'), may hold values from 0.099609375 to 1.8984375
- w_query: bfloat16 [2048, 2048], P('fsdp', 'tp'), may hold values from -0.125 to 0.125
- w_key: bfloat16 [2048, 256], P('fsdp', 'tp'), may hold values from -0.125 to 0.125
- w_value: bfloat16 [2048, 256], P('fsdp', 'tp'), may hold values from -0.125 to 0.125
- w_out: bfloat16 [2048, 2048], P('tp', 'fsdp'), may hold values from -1 to 1
- mlp_gain: bfloat16 [2048], P('fsdp'), may hold values from 0.099609375 to 1.8984375
- w_gate: bfloat16 [2048, 5632], P('fsdp', 'tp'), may hold values from -0.125 to 0.125
- w_up: bfloat16 [2048, 5632], P('fsdp', 'tp'), may hold values from -0.125 to 0.125
- w_down: bfloat16 [5632, 2048], P('tp', 'fsdp'), may hold values from -0.078125 to 0.078125
Outputs:
- output: bfloat16 [4, 1024, 2048], P('fsdp', 'ctx')
- input_grad: float32 [4, 1024, 2048], P('fsdp', 'ctx')
- attn_gain_grad: float32 [2048], P('fsdp')
- query_grad: float32 [2048, 2048], P('fsdp', 'tp')
- key_grad: float32 [2048, 256], P('fsdp', 'tp')
- value_grad: float32 [2048, 256], P('fsdp', 'tp')
- out_grad: float32 [2048, 2048], P('tp', 'fsdp')
- mlp_gain_grad: float32 [2048], P('fsdp')
- gate_grad: float32 [2048, 5632], P('fsdp', 'tp')
- up_grad: float32 [2048, 5632], P('fsdp', 'tp')
- down_grad: float32 [5632, 2048], P('tp', 'fsdp')
Inputs may be any that keep to these rules, and one draw needn't show every extreme that they name: `positions`: positions start at 0 and rise by 1 or 2 from each token to the next along a sequence; in every sequence exactly 512 of these steps are 2. `blocks`: block ids never fall along a sequence; every block holds 1 to 256 tokens.
All inputs are finite; a program needn't handle non-finite values.
Results may differ from a plain program's by a relative error of at most 0.023.
Values may be sent and summed in bfloat16 or wider, within the bound.
A program may use at most 320 MiB of HBM per device.

v0:
```python
import functools
import math

import jax
import jax.numpy as jnp
from jax import lax
from jax.experimental import pallas as pl
from jax.experimental.pallas import tpu as pltpu
from jax.sharding import PartitionSpec as P

HD = 64
EPSILON = 1e-05
NEGATIVE = -1e30
BF = jnp.bfloat16
F32 = jnp.float32


def dot(a, b, ca, cb):
    return lax.dot_general(a, b, (((ca,), (cb,)), ((), ())), preferred_element_type=F32)


def angles(positions):
    half = HD // 2
    frequency = jnp.exp(jnp.arange(half, dtype=F32) * (-2.0 * math.log(10000.0) / HD))
    turned = positions.astype(F32)[:, None] * frequency[None, :]
    return jnp.cos(turned)[:, None, :], jnp.sin(turned)[:, None, :]


def rotate(values, cosine, sine):
    half = HD // 2
    a, b = values[..., :half], values[..., half:]
    return jnp.concatenate([a * cosine - b * sine, b * cosine + a * sine], axis=-1)


def gated(values, after):
    return lax.optimization_barrier((values, after))[0]


def local(n, m, inputs, positions, blocks, cotangent, attn_gain, w_query, w_key, w_value, w_out, mlp_gain, w_gate, w_up, w_down):
    f = lax.axis_index("fsdp")
    z = lax.axis_index("ctx")
    t = lax.axis_index("tp")
    tokens, width = inputs.shape[1:]
    half = width // 2
    peers = range(1, n)

    def plane(x, k):
        return x if k == 0 else lax.ppermute(x, "fsdp", [(i, i ^ k) for i in range(n)])

    def column(x, k):
        return x if k == 0 else lax.ppermute(x, "ctx", [(i, i ^ k) for i in range(m)])

    def swap(x):
        return lax.ppermute(x, "tp", [(0, 1), (1, 0)])

    def part(x, index, axis):
        size = x.shape[axis] // n
        return lax.dynamic_slice_in_dim(x, index * size, size, axis)

    def mine(x, which):
        return lax.dynamic_slice_in_dim(x, which * half, half, x.ndim - 1)

    def place(pieces, axis):
        size = pieces[0].shape[axis]
        shape = list(pieces[0].shape)
        shape[axis] = size * n
        whole = jnp.zeros(shape, pieces[0].dtype)
        for k in range(n):
            whole = lax.dynamic_update_slice_in_dim(whole, pieces[k], (f ^ k) * size, axis)
        return whole

    def join(own, other):
        return jnp.where(t == 0, jnp.concatenate([own, other], -1), jnp.concatenate([other, own], -1))

    def gather(x):
        rows = jnp.concatenate([plane(x, k) for k in range(n)], 0)
        return join(rows, swap(rows))

    def scatter(partial):
        own = mine(partial, t) + swap(mine(partial.astype(BF), 1 - t)).astype(F32)
        low = own.astype(BF)
        total = own[:tokens]
        for k in peers:
            total = total + plane(low[k * tokens : (k + 1) * tokens], k).astype(F32)
        return total

    def row_mean(own):
        own = jnp.sum(own, -1)
        return ((own + swap(own)) / width)[:, None]

    x = inputs[0].astype(F32)
    gains = jnp.stack([attn_gain, mlp_gain])
    gains = place([plane(gains, k) for k in range(n)], 1).astype(F32)
    marks = jnp.stack([positions[0], blocks[0]])
    marks = [plane(marks, k) for k in range(n)]
    place_rows = jnp.concatenate([mk[0] for mk in marks])
    query_ids = jnp.stack([mk[1] for mk in marks])
    scale_one = lax.rsqrt(jnp.mean(x * x, axis=-1, keepdims=True) + EPSILON)
    x_half = mine(x, t)
    hat_one = x_half * scale_one
    gain_one, gain_two = mine(gains[0:1], t), mine(gains[1:2], t)
    xn_one = gather((hat_one * gain_one).astype(BF))

    heads = w_query.shape[1] // HD // n
    cols = heads * HD
    kv_pair = jnp.concatenate([w_key, w_value], 1)
    kv_heads = w_key.shape[1] // HD
    w_qkv = place([plane(jnp.concatenate([part(w_query, f ^ k, 1), kv_pair], 1), k) for k in range(n)], 0)
    wo = gated(w_out, xn_one)
    wo = place([plane(part(wo, f ^ k, 0), k) for k in range(n)], 1)
    gate_up = gated((w_gate, w_up), xn_one)
    gate_up = [plane(jnp.stack([part(gate_up[0], f ^ k, 1), part(gate_up[1], f ^ k, 1)]), k) for k in range(n)]
    wg = place([g[0] for g in gate_up], 0)
    wu = place([g[1] for g in gate_up], 0)

    qkv = dot(xn_one, w_qkv, 1, 0)
    cosine, sine = angles(place_rows)
    kv_here = (heads * f) // ((w_query.shape[1] // HD) // kv_heads)

    def pick(both):
        out = both[:, :HD]
        for g in range(1, kv_heads):
            out = jnp.where(kv_here == g, both[:, g * HD : (g + 1) * HD], out)
        return out

    kw = kv_heads * HD
    query = rotate(qkv[:, :cols].reshape(-1, heads, HD), cosine, sine).astype(BF)
    key = rotate(pick(qkv[:, cols : cols + kw])[:, None, :], cosine, sine)[:, 0, :].astype(BF)
    value = pick(qkv[:, cols + kw :]).astype(BF)
    key_value = jnp.concatenate([key, value], 1).reshape(n, tokens, 2 * HD)
    kv_all = jnp.concatenate([column(key_value, k) for k in range(m)], 1)
    ids_all = jnp.concatenate([column(query_ids, k) for k in range(m)], 1)
    keys, values = kv_all[..., :HD], kv_all[..., HD:]
    factor = 1.0 / math.sqrt(HD)
    query = query.reshape(n, tokens, heads, HD)
    allowed = (ids_all[:, None, :] <= query_ids[:, :, None])[:, None]
    scores = jnp.einsum("nthd,nsd->nhts", query, keys, preferred_element_type=F32) * factor
    scores = jnp.where(allowed, scores, NEGATIVE)
    top = jnp.max(scores, -1, keepdims=True)
    raw = jnp.where(allowed, jnp.exp(scores - top), 0.0)
    weights = raw / jnp.sum(raw, -1, keepdims=True)
    weights_low = weights.astype(BF)
    attended = jnp.einsum("nhts,nsd->nthd", weights_low, values, preferred_element_type=F32)
    attended_low = attended.astype(BF).reshape(n * tokens, cols)

    hidden = x_half + scatter(dot(attended_low, wo, 1, 0))
    scale_two = lax.rsqrt(row_mean(hidden * hidden) + EPSILON)
    hat_two = hidden * scale_two
    xn_two = gather((hat_two * gain_two).astype(BF))
    cot = gather(gated(mine(cotangent[0], t), wg))
    wd = gated(w_down, wg)
    wd = place([plane(part(wd, f ^ k, 0), k) for k in range(n)], 1)
    gate = dot(xn_two, wg, 1, 0)
    up = dot(xn_two, wu, 1, 0)
    sigma = jax.nn.sigmoid(gate)
    silu = gate * sigma
    act = (silu * up).astype(BF)
    dact = dot(cot, wd, 1, 1)
    dgate = (dact * up * sigma * (1.0 + gate * (1.0 - sigma))).astype(BF)
    dup = (dact * silu).astype(BF)

    def reduce(piece):
        if m != 4:
            return lax.psum(piece, "ctx")
        one = (piece.astype(F32) + lax.ppermute(piece, "ctx", [(0, 1), (3, 2)]).astype(F32)).astype(BF)
        two = (one.astype(F32) + lax.ppermute(one, "ctx", [(1, 2), (2, 1)]).astype(F32)).astype(BF)
        three = lax.ppermute(two, "ctx", [(1, 0), (2, 3)])
        return jnp.where((z == 0) | (z == 3), three, two)

    def share(grad, axis):
        low = grad.astype(BF)
        return [plane(part(low, f ^ k, axis), k) for k in range(n)]

    down_parts = [reduce(p) for p in share(dot(act, cot, 0, 0), 1)]
    gate_parts = [reduce(p) for p in share(dot(xn_two, dgate, 0, 0), 0)]
    up_parts = [reduce(p) for p in share(dot(xn_two, dup, 0, 0), 0)]
    d_two = scatter(dot(dgate, wg, 1, 1) + dot(dup, wu, 1, 1))
    out_half = (hidden + scatter(dot(act, wd, 1, 0))).astype(BF)
    output = join(out_half, swap(out_half))
    gain_two_grad = jnp.sum(d_two * hat_two, 0)
    e_two = d_two * gain_two
    d_hidden = mine(cotangent[0], t).astype(F32) + scale_two * (e_two - hat_two * row_mean(e_two * hat_two))
    dhb = gather(d_hidden.astype(BF))
    out_parts = [reduce(p) for p in share(dot(attended_low, dhb, 0, 0), 1)]

    d_att = dot(dhb, wo, 1, 1).astype(BF).reshape(n, tokens, heads, HD)
    delta = jnp.einsum("nthd,nthd->nht", d_att.astype(F32), attended)
    d_weights = jnp.einsum("nthd,nsd->nhts", d_att, values, preferred_element_type=F32)
    d_scores = (weights * (d_weights - delta[..., None])).astype(BF)
    dv = jnp.einsum("nhts,nthd->nsd", weights_low, d_att, preferred_element_type=F32)
    dk = jnp.einsum("nhts,nthd->nsd", d_scores, query, preferred_element_type=F32) * factor
    dq = jnp.einsum("nhts,nsd->nthd", d_scores, keys, preferred_element_type=F32) * factor
    d_kv = jnp.concatenate([dk, dv], -1).reshape(n, m, tokens, 2 * HD)
    d_low = d_kv.astype(BF)
    d_kv_own = d_kv[:, 0]
    for k in range(1, m):
        d_kv_own = d_kv_own + column(d_low[:, k], k).astype(F32)
    d_kv_own = d_kv_own.reshape(n * tokens, 2 * HD)
    dq = rotate(dq.reshape(n * tokens, heads, HD), cosine, -sine).reshape(n * tokens, cols)
    dk = rotate(d_kv_own[:, None, :HD], cosine, -sine)[:, 0, :]
    d_qkv = jnp.concatenate([dq, dk, d_kv_own[:, HD:]], 1).astype(BF)
    w_here = jnp.concatenate([w_qkv[:, :cols], pick(w_qkv[:, cols : cols + kw]), pick(w_qkv[:, cols + kw :])], 1)
    d_one = scatter(dot(d_qkv, w_here, 1, 1))
    qkv_parts = share(dot(xn_one, d_qkv, 0, 0), 0)
    key_parts, value_parts = [0.0] * kv_heads, [0.0] * kv_heads
    for k in range(n):
        owner = (heads * (f ^ k)) // ((w_query.shape[1] // HD) // kv_heads)
        piece = qkv_parts[k].astype(F32)
        for g in range(kv_heads):
            key_parts[g] = key_parts[g] + jnp.where(owner == g, piece[:, cols : cols + HD], 0.0)
            value_parts[g] = value_parts[g] + jnp.where(owner == g, piece[:, cols + HD :], 0.0)
    small = reduce(jnp.concatenate(key_parts + value_parts, 1).astype(BF)).astype(F32)
    query_parts = [reduce(p[:, :cols]) for p in qkv_parts]
    gain_one_grad = jnp.sum(d_one * hat_one, 0)
    e_one = d_one * gain_one
    in_half = d_hidden + scale_one * (e_one - hat_one * row_mean(e_one * hat_one))
    input_grad = join(in_half, swap(in_half))
    gain_grads = jnp.stack([gain_one_grad, gain_two_grad])
    nothing = jnp.zeros_like(gain_grads)
    gain_grads = jnp.where(t == 0, jnp.concatenate([gain_grads, nothing], 1), jnp.concatenate([nothing, gain_grads], 1))
    gain_grads = part(lax.psum(gain_grads, ("fsdp", "ctx", "tp")), f, 1)

    def settle(pieces, axis):
        return place(pieces, axis).astype(F32)

    return (
        output[None],
        input_grad[None],
        gain_grads[0],
        settle(query_parts, 1),
        small[:, :kw],
        small[:, kw:],
        settle(out_parts, 0),
        gain_grads[1],
        settle(gate_parts, 1),
        settle(up_parts, 1),
        settle(down_parts, 0),
    )


T, W, H, TILE = 256, 2048, 1024, 128
MAIN, WIN = 640, 768
GRADS = (("d", 2816, 512), ("g", 512, 2816), ("u", 512, 2816), ("o", 1024, 512), ("q", 512, 1024), ("k", 512, 256))
PART = 384


PARTS = {"dA": (0, 128), "dB": (128, 256), "dC": (PART, PART)}
PARTS |= {name + which: (0 if which == "A" else PART, PART) for name in "gu" for which in "AB"}
LAST = ("dC", "gB", "uB")
GROUPS = tuple(PARTS) + ("o", "q", "k")


def chunk_list():
    chunks = []
    for group, (_, size) in PARTS.items():
        for j in range(4):
            part = MAIN - PART if group in LAST and j % 2 else size
            chunks.append((group, group[0], j, j) + ((part, 512) if group[0] == "d" else (512, part)))
    chunks += [("o", "o", r, 0, 256, 512) for r in range(0, 1024, 256)]
    chunks += [("q", "q", 0, c, 512, 256) for c in range(0, 1024, 256)]
    return chunks + [("k", "k", r, 0, 256, 256) for r in (0, 256)]


CHUNKS = chunk_list()
DEPTH = 4
ORDER = (
    "dA", "+", "feed_back", 1, 1, 1, "dB", "gate_A", 1, 1, "d2_first", 1, "d2_own", 1, "dC", "relay", 1, 1, "gate_B", "gA", 1,
    "norm_two_back", 1, 1, 1, "gB", "up_A", 1, 1, "dh_take", "+", "out_grads", 1, "attend0", 1, "attend1", 1, "uA", "+", "up_B", 1, "attend2", 1,
    "attend3", "pair_send", 1, "-", "pair_sum", "uB", "+", 1, "o", "d_kv_take", 1, "qkv_grads", 1, "d1_first", 1, "d1_own", 1, "q", 1, "relay", 1,
    "kv_ready", 1, 1, "norm_one_back", 1, "out_first", 1, "out_own", 1, "relay", 1, "-", "gains_column", "-", "out_end", "gains_end",
)
MESH = pl.DeviceIdType.MESH


def nn(a, b):
    return lax.dot_general(a, b, (((1,), (0,)), ((), ())), preferred_element_type=F32)


def nt(a, b):
    return lax.dot_general(a, b, (((1,), (1,)), ((), ())), preferred_element_type=F32)


def tn(a, b):
    return lax.dot_general(a, b, (((0,), (0,)), ((), ())), preferred_element_type=F32)


def flip(a, k):
    return (a % 2 + k % 2) % 2 + 2 * ((a // 2 + k // 2) % 2)


def layer_kernel(*refs):
    names = iter(refs)

    def take(count):
        return [next(names) for _ in range(count)]

    x_in, table_in, gains_in, cot_in, wq, wk, wv, wo, wg, wu, wd = take(11)
    out_ref, in_grad_ref, gain_ref = take(3)
    first, left, cross, total = ({name: next(names) for name, _, _ in GRADS} for _ in range(4))
    (x1, x2, ct, dh, w_qkv, w_o, w_g, w_u, w_d, act, dg, du, q_buf, kv_all, ob) = take(15)
    (ps, pr, rr, rd, yo, hid, d_hid, xv, tb, ga, ids, r1s, r2s, ss_own, ss_other, lse, bias) = take(17)
    (gs_d, kv_g, line, d_kv, d_kv_pair, d_kv_recv, out_s, g_sum, g_plane, g_column, g_whole) = take(11)
    send_sem, recv_sem, local_sem, credit = take(4)
    f, z, t = lax.axis_index("fsdp"), lax.axis_index("ctx"), lax.axis_index("tp")
    sems = iter(range(10**6))
    drains = []

    def al(v, by):
        return pl.multiple_of(v, by)

    def plane(k):
        return (flip(f, k), z, t)

    def column(k):
        return (f, flip(z, k), t)

    core = (f, z, 1 - t)
    rows_f = pl.ds(al(f * T, T), T)
    half = pl.ds(al(t * H, H), H)
    rest = pl.ds(al((1 - t) * H, H), H)

    def rows_of(b):
        return pl.ds(al(b * T, T), T)

    def remote(src, dst, s, device):
        return pltpu.make_async_remote_copy(src_ref=src, dst_ref=dst, send_sem=send_sem.at[s], recv_sem=recv_sem.at[s], device_id=device, device_id_type=MESH)

    def here(src, dst, s):
        return pltpu.make_async_copy(src, dst, local_sem.at[s])

    local_count = iter(range(10**6))

    lx = here(x_in.at[0], xv, next(local_count))
    lx.start()
    lc = here(cot_in.at[0], ct.at[rows_f, :], next(local_count))
    lc.start()
    lh = here(cot_in.at[0, :, half], out_s, next(local_count))
    lh.start()
    lt = here(table_in, tb.at[f], next(local_count))
    lt.start()
    lg = here(gains_in, ga.at[:, pl.ds(al(f * 512, 512), 512)], next(local_count))
    lg.start()

    def starts(r):
        return (11 * r + 1 - t) // 2

    def full(r):
        return (r + t) % 2 == 0

    def weight_moves(k, taking):
        r = flip(f, k)
        sender, taker = (r, f) if taking else (f, r)
        rows = pl.ds(al(sender * 512, 512), 512)
        row_part = pl.ds(al(sender * 512 + z * TILE, TILE), TILE)
        own_part = pl.ds(al(z * TILE, TILE), TILE)
        begin = al(starts(taker) * TILE, TILE)
        tail = al(begin + MAIN, TILE)
        col = al(taker * T, T)
        moves = {
            "o": [(wo.at[pl.ds(col, T), :], w_o.at[:, rows])],
            "g": [(wg.at[:, pl.ds(begin, MAIN)], w_g.at[rows, pl.ds(0, MAIN)])],
            "g+": [(wg.at[:, pl.ds(tail, TILE)], w_g.at[rows, pl.ds(MAIN, TILE)])],
        }
        from_rows, to_rows = pl.ds(0, 512), rows
        if k:
            from_rows, to_rows = pl.ds(al(z % 2 * T, T), T), pl.ds(al(sender * 512 + z % 2 * T, T), T)
        moves["qkv"] = [
            (wq.at[from_rows, pl.ds(col, T)], w_qkv.at[to_rows, pl.ds(0, T)]),
            (wk.at[from_rows, :], w_qkv.at[to_rows, pl.ds(T, TILE)]),
            (wv.at[from_rows, :], w_qkv.at[to_rows, pl.ds(T + TILE, TILE)]),
        ]
        if k == 0:
            moves["u"] = [(wu.at[:, pl.ds(begin, MAIN)], w_u.at[rows, pl.ds(0, MAIN)])]
            moves["u+"] = [(wu.at[:, pl.ds(tail, TILE)], w_u.at[rows, pl.ds(MAIN, TILE)])]
            moves["d"] = [(wd.at[pl.ds(begin, MAIN), :], w_d.at[pl.ds(0, MAIN), rows])]
            moves["d+"] = [(wd.at[pl.ds(tail, TILE), :], w_d.at[pl.ds(MAIN, TILE), rows])]
        else:
            moves["u"] = [(wu.at[own_part, pl.ds(begin, MAIN)], w_u.at[row_part, pl.ds(0, MAIN)])]
            moves["u+"] = [(wu.at[own_part, pl.ds(tail, TILE)], w_u.at[row_part, pl.ds(MAIN, TILE)])]
            moves["d"] = [(wd.at[pl.ds(begin, MAIN), own_part], w_d.at[pl.ds(0, MAIN), row_part])]
            moves["d+"] = [(wd.at[pl.ds(tail, TILE), own_part], w_d.at[pl.ds(MAIN, TILE), row_part])]
        return moves

    w_counts = (("qkv", 3), ("o", 1), ("g", 1), ("g+", 1), ("u", 1), ("u+", 1), ("d", 1), ("d+", 1))
    w_sem = {(key, k, i): next(sems) for key, c in w_counts for k in (1, 2, 3) for i in range(c)}
    w_local = {(key, i): next(local_count) for key, c in w_counts for i in range(c)}

    def weights_each(key, taking, run):
        for k in (1, 2, 3):
            moves = weight_moves(k, taking)
            for i, (src, dst) in enumerate(moves[key]):
                run(remote(src, dst, w_sem[key, k, i], plane(k)))
            if key + "+" in moves:

                @pl.when(full(f if taking else flip(f, k)))
                def _():
                    (src, dst), = moves[key + "+"]
                    run(remote(src, dst, w_sem[key + "+", k, 0], plane(k)))

    def weights_start(key):
        weights_each(key, False, lambda cp: cp.start())

    def weights_wait(key):
        weights_each(key, True, lambda cp: cp.wait_recv())

    def weights_drain():
        for key in ("qkv", "o", "g", "u", "d"):
            weights_each(key, False, lambda cp: cp.wait_send())

    def weights_own(keys, wait):
        moves = weight_moves(0, False)

        def run(key):
            for i, (src, dst) in enumerate(moves[key]):
                cp = here(src, dst, w_local[key, i])
                cp.wait() if wait else cp.start()

        for key in keys:
            run(key)
            if key + "+" in moves:
                pl.when(full(f))(functools.partial(run, key + "+"))

    y_sem = {(key, k, j): next(sems) for key in ("qkv", "u", "d") for k in (1, 2, 3) for j in (1, 2, 3) if key != "qkv" or j == 1}

    def column_each(key, taking, run):
        for k in (1, 2, 3):
            for j in (1, 2, 3):
                from_z = flip(z, j) if taking else z
                part = pl.ds(al(flip(f, k) * 512 + from_z * TILE, TILE), TILE)

                def move(size):
                    ref = w_u.at[part, pl.ds(0, size)] if key == "u" else w_d.at[pl.ds(0, size), part]
                    run(remote(ref, ref, y_sem[key, k, j], column(j)))

                if key == "qkv":
                    if j == 1:
                        ref = w_qkv.at[pl.ds(al(flip(f, k) * 512 + from_z % 2 * T, T), T), :]
                        run(remote(ref, ref, y_sem[key, k, j], column(j)))
                    continue
                pl.when(full(f))(functools.partial(move, WIN))
                pl.when(full(f + 1))(functools.partial(move, MAIN))

    g_sem = [[next(sems) for _ in range(4)] for _ in range(4)]
    f_sem = [[next(sems) for _ in range(4)] for _ in range(4)]
    quarters = (pl.ds(al(t * H, 512), 512), pl.ds(al(t * H + 512, 512), 512))

    def gather_direct(g):
        return (1, 2, 3) if g == 3 else (1, 2)

    def gather_start(g, buf, with_own, src=None):
        block = buf.at[rows_f, half]
        for k in gather_direct(g):
            remote(block if src is None else src, block, g_sem[g][k - 1], plane(k)).start()
        if with_own:
            remote(block, block, f_sem[g][3], core).start()

    def gather_hand(g, buf, k):
        block = buf.at[rows_of(flip(f, k)), half]
        return remote(block, block, f_sem[g][k - 1], core)

    def gather_relay(g, buf, k):
        part = buf.at[rows_of(flip(f, k)), quarters[k - 1]]
        return remote(part, part, g_sem[g][4 - k], plane(3 - k))

    def gather_forward(g, buf):
        for k in gather_direct(g):
            block = buf.at[rows_of(flip(f, k)), half]
            remote(block, block, g_sem[g][k - 1], plane(k)).wait_recv()
            if g != 3:
                gather_relay(g, buf, k).start()
            gather_hand(g, buf, k).start()

    def gather_diagonal(g, buf):
        for k in (1, 2):
            part = buf.at[rows_of(flip(f, 3)), quarters[k - 1]]
            remote(part, part, g_sem[g][4 - k], plane(3 - k)).wait_recv()
        gather_hand(g, buf, 3).start()

    def gather_take(g, buf, k):
        if k == 0:
            block = buf.at[rows_f, rest]
            remote(block, block, f_sem[g][3], core).wait_recv()
        else:
            block = buf.at[rows_of(flip(f, k)), rest]
            remote(block, block, f_sem[g][k - 1], core).wait_recv()

    def gather_drain(g, buf, with_own, src=None):
        block = buf.at[rows_f, half]
        for k in gather_direct(g):
            remote(block if src is None else src, block, g_sem[g][k - 1], plane(k)).wait_send()
        for k in (1, 2, 3):
            gather_hand(g, buf, k).wait_send()
            if g != 3 and k != 3:
                gather_relay(g, buf, k).wait_send()
        if with_own:
            remote(block, block, f_sem[g][3], core).wait_send()

    t_sem = [next(sems) for _ in range(3)]
    a_sem = [next(sems) for _ in range(3)]
    own_gain = ga.at[:, pl.ds(al(f * 512, 512), 512)]

    barrier = pltpu.get_barrier_semaphore()
    for k in (1, 2, 3):
        pl.semaphore_signal(barrier, inc=1, device_id=plane(k), device_id_type=MESH)
        pl.semaphore_signal(barrier, inc=1, device_id=column(k), device_id_type=MESH)
    pl.semaphore_signal(barrier, inc=1, device_id=core, device_id_type=MESH)
    pl.semaphore_wait(barrier, 7)

    lt.wait()
    lg.wait()
    for k in (1, 2, 3):
        remote(own_gain, own_gain, a_sem[k - 1], plane(k)).start()
        remote(tb.at[f], tb.at[f], t_sem[k - 1], plane(k)).start()
    weights_start("qkv")
    weights_own(("qkv",), False)

    @pl.when(full(f + 1))
    def _():
        w_g[:, MAIN:WIN] = jnp.zeros((W, TILE), BF)
        w_u[:, MAIN:WIN] = jnp.zeros((W, TILE), BF)
        w_d[MAIN:WIN, :] = jnp.zeros((TILE, W), BF)

    lx.wait()
    for k in (1, 2, 3):
        dst = ga.at[:, pl.ds(al(flip(f, k) * 512, 512), 512)]
        remote(dst, dst, a_sem[k - 1], plane(k)).wait_recv()

    STEP = 32

    def sub(i):
        return pl.ds(al(i * STEP, STEP), STEP)

    @pl.loop(0, T // STEP)
    def _(i):
        xs = xv[sub(i), :].astype(F32)
        scale = lax.rsqrt(jnp.mean(xs * xs, axis=-1, keepdims=True) + EPSILON)
        r1s[sub(i), :] = jnp.broadcast_to(scale, (STEP, TILE))
        x1[pl.ds(al(f * T + i * STEP, STEP), STEP), :] = (xs * scale * ga[0:1, :]).astype(BF)

    weights_wait("qkv")
    column_each("qkv", False, lambda cp: cp.start())
    gather_start(0, x1, False)
    gather_forward(0, x1)
    for key in "oudg":
        weights_start(key)
    weights_own("oudg", False)
    gather_diagonal(0, x1)
    for k in (1, 2, 3):
        dst = tb.at[flip(f, k)]
        remote(dst, dst, t_sem[k - 1], plane(k)).wait_recv()
    weights_own(("qkv",), True)
    column_each("qkv", True, lambda cp: cp.wait_recv())

    lane = lax.broadcasted_iota(jnp.int32, (T, TILE), 1)
    low_lane = lane < HD
    first_half = lane % HD < HD // 2
    kv_head = f // 2

    def turns(b):
        cosine, sine = tb[b, 0:32, :], tb[b, 32:64, :]
        return (
            jnp.transpose(jnp.concatenate([cosine] * 4, 0)),
            jnp.transpose(jnp.concatenate([-sine, sine, -sine, sine], 0)),
        )

    def turn(v, c, s):
        swapped = jnp.where(first_half, pltpu.roll(v, TILE - 32, 1), pltpu.roll(v, 32, 1))
        return v * c + swapped * s

    def qkv_block(k):
        b = flip(f, k)
        qkv = nn(x1[rows_of(b), :], w_qkv[...])
        c, s = turns(b)
        for i in range(2):
            q = turn(qkv[:, i * TILE : (i + 1) * TILE], c, s) * 0.125
            q_buf[rows_of(b), i * TILE : (i + 1) * TILE] = q.astype(BF)
        key = turn(qkv[:, 2 * TILE : 3 * TILE], c, s)
        value = qkv[:, 3 * TILE :]
        key = jnp.where(kv_head == 0, key, pltpu.roll(key, HD, 1))
        value = jnp.where(kv_head == 1, value, pltpu.roll(value, HD, 1))
        kv_all[z, b, :, :] = jnp.where(low_lane, key, value).astype(BF)
        ids[z, pl.ds(b, 1), :] = tb[b, 64:65, :]

    qkv_block(0)
    for k in (1, 2, 3):
        gather_take(0, x1, k)

    @pl.loop(1, 4)
    def _(k):
        qkv_block(k)

    z_sem = [[next(sems) for _ in range(2)] for _ in range(3)]
    for k in (1, 2, 3):
        remote(kv_all.at[z], kv_all.at[z], z_sem[k - 1][0], column(k)).start()
        remote(ids.at[z], ids.at[z], z_sem[k - 1][1], column(k)).start()
    for k in (1, 2, 3):
        zz = flip(z, k)
        remote(kv_all.at[zz], kv_all.at[zz], z_sem[k - 1][0], column(k)).wait_recv()
        remote(ids.at[zz], ids.at[zz], z_sem[k - 1][1], column(k)).wait_recv()
    lc.wait()
    weights_wait("u")
    column_each("u", False, lambda cp: cp.start())

    low_keys = lax.broadcasted_iota(jnp.int32, (4 * T, TILE), 1) < HD

    def bias_of(s):
        query_id = ids[z, pl.ds(s, 1), :]
        for j in range(4):
            key_id = jnp.transpose(jnp.broadcast_to(ids[j, pl.ds(s, 1), :], (8, T)))[:, 0:1]
            bias[j * T : (j + 1) * T, :] = jnp.where(key_id <= query_id, 0.0, NEGATIVE).astype(BF)

    def kv_of(s):
        kv = jnp.concatenate([kv_all[j, s, :, :] for j in range(4)], 0).astype(F32)
        turned = pltpu.roll(kv, HD, 1)
        keys = jnp.where(low_keys, kv, turned).astype(BF)
        values = jnp.where(low_keys, turned, kv).astype(BF)
        return kv, keys, values

    def only(v, parity):
        return jnp.where(low_lane if parity == 0 else ~low_lane, v.astype(F32), 0.0).astype(BF)

    @pl.loop(0, 4)
    def _(s):
        bias_of(s)
        kv, keys, _ = kv_of(s)
        values_t = jnp.transpose(kv)[HD:, :].astype(BF)

        for i in range(2):
            mixed = []
            for parity in range(2):
                q = only(q_buf[rows_of(s), i * TILE : (i + 1) * TILE], parity)
                scores = nt(keys, q) + bias[...].astype(F32)
                top = jnp.max(scores, axis=0, keepdims=True)
                raw = jnp.exp(scores - top)
                norm = jnp.sum(raw, axis=0, keepdims=True)
                lse[s, 2 * i + parity : 2 * i + parity + 1, :] = top + jnp.log(norm)
                mixed.append(nn(values_t, raw.astype(BF)) * (1.0 / norm))
            ob[rows_of(s), i * TILE : (i + 1) * TILE] = jnp.transpose(jnp.concatenate(mixed, 0)).astype(BF)

    p_sem = [next(sems) for _ in range(4)][0]
    s_sem = [next(sems) for _ in range(6)]
    COLS = 256
    lows, highs = pl.ds(0, 512), pl.ds(512, 512)

    def pass_first(k):
        return remote(ps.at[3, :, (lows, highs)[k - 1]], rd.at[k - 1], s_sem[k - 1], plane(k))

    def pass_second(k, added):
        cols = (lows, highs)[k - 1 if not added else 2 - k]
        return remote(ps.at[k, :, cols], rr.at[k - 1, :, cols], s_sem[2 * k + added], plane(k))

    def tiles(run):
        @pl.loop(0, H // COLS)
        def _(j):
            run(pl.ds(al(j * COLS, COLS), COLS), j * COLS)

    def core_move(k):
        return remote(ps.at[k], pr.at[k], p_sem + k, core)

    def scatter_first(product):
        @pl.loop(0, 4)
        def _(i):
            k = (7 - i) % 4

            def run(cols, c):
                ps[k, :, cols] = product(flip(f, k), (1 - t) * H + c).astype(BF)

            tiles(run)
            core_move(k).start()

    def scatter_own(product):
        @pl.loop(0, 3)
        def _(i):
            k = (i + 2) % 3 + 1
            core_move(k).wait()

            def run(cols, c):
                ps[k, :, cols] = (product(flip(f, k), t * H + c) + pr[k, :, cols].astype(F32)).astype(BF)

            tiles(run)

            @pl.when(k == 3)
            def _():
                pass_first(1).start()
                pass_first(2).start()

        pass_second(1, 0).start()
        pass_second(2, 0).start()
        core_move(0).wait()

        def run(cols, c):
            yo[:, cols] = product(f, t * H + c) + pr[0, :, cols].astype(F32)

        tiles(run)

    def scatter_steps(product):
        return functools.partial(scatter_first, product), functools.partial(scatter_own, product)

    def scatter_relay():
        for k in (1, 2):
            pass_first(3 - k).wait()
            c = (512, 0)[k - 1]

            @pl.loop(0, T // STEP)
            def _(i):
                ps[k, sub(i), c : c + 512] = (ps[k, sub(i), c : c + 512].astype(F32) + rd[2 - k, sub(i), :].astype(F32)).astype(BF)

            pass_second(k, 1).start()

    def scatter_wait():
        for k in (1, 2):
            for added in (0, 1):
                pass_second(k, added).wait()

    def scattered(i):
        return yo[sub(i), :] + rr[0, sub(i), :].astype(F32) + rr[1, sub(i), :].astype(F32)

    n_sem = [next(sems) for _ in range(3)]

    def core_sums(u):
        remote(ss_own.at[u], ss_other.at[u], n_sem[u], core).start()
        remote(ss_own.at[u], ss_other.at[u], n_sem[u], core).wait()

    weights_wait("o")
    weights_own("o", True)
    for step in scatter_steps(lambda b, c: nn(ob[rows_of(b), :], w_o[:, pl.ds(al(c, COLS), COLS)])):
        step()
    scatter_relay()
    scatter_wait()
    weights_wait("d")
    column_each("d", False, lambda cp: cp.start())

    @pl.loop(0, T // STEP)
    def _(i):
        rows = xv[sub(i), half].astype(F32) + scattered(i)
        hid[sub(i), :] = rows
        ss_own[0, sub(i), :] = jnp.broadcast_to(jnp.sum(rows * rows, axis=-1, keepdims=True), (STEP, TILE))

    core_sums(0)
    gain_one, gain_two = ga[0:1, half], ga[1:2, half]

    @pl.loop(0, T // STEP)
    def _(i):
        scale = lax.rsqrt((ss_own[0, sub(i), 0:1] + ss_other[0, sub(i), 0:1]) * (1.0 / W) + EPSILON)
        r2s[sub(i), :] = jnp.broadcast_to(scale, (STEP, TILE))
        x2[pl.ds(al(f * T + i * STEP, STEP), STEP), half] = (hid[sub(i), :] * scale * gain_two).astype(BF)

    gather_start(2, x2, True)
    gather_forward(2, x2)
    gather_start(1, ct, False, cot_in.at[0, :, half])
    weights_wait("g")
    weights_own("ugd", True)
    column_each("u", True, lambda cp: cp.wait_recv())

    UNITS = 256

    def feed_block(k):
        b = flip(f, k)

        @pl.loop(0, WIN // UNITS)
        def _(j):
            cols = pl.ds(al(j * UNITS, UNITS), UNITS)
            gate = nn(x2[rows_of(b), :], w_g[:, cols])
            up = nn(x2[rows_of(b), :], w_u[:, cols])
            sigma = jax.nn.sigmoid(gate)
            silu = gate * sigma
            act[rows_of(b), cols] = (silu * up).astype(BF)
            dg[rows_of(b), cols] = (up * sigma * (1.0 + gate * (1.0 - sigma))).astype(BF)
            du[rows_of(b), cols] = silu.astype(BF)

    for k in (0, 1, 2):
        gather_take(2, x2, k)

    @pl.loop(0, 3)
    def _(k):
        feed_block(k)

    gather_diagonal(2, x2)
    gather_take(2, x2, 3)
    feed_block(3)
    gather_forward(1, ct)
    gather_diagonal(1, ct)
    for k in (1, 2, 3):
        gather_take(1, ct, k)

    e_sem = {(name, i): [next(sems) for _ in range(3)][0] for name in GROUPS for i in range(2 if name in LAST else 1)}
    e_local = {(name, i): next(local_count) for name in GROUPS for i in range(2 if name in LAST else 1)}

    def stage(name, k):
        if name == "d":
            return gs_d.at[pl.ds(al(k * WIN, WIN), WIN), :]
        if name in "gu":
            return ct.at[pl.ds(al((k // 2) * 512, 512), 512), pl.ds(al((k % 2) * H, H), WIN)]
        if name == "o":
            return gs_d.at[pl.ds(al(k * WIN, WIN), T), :]
        return x2.at[pl.ds(al((k // 2) * 512, 512), 512), pl.ds(al((k % 2) * 512 + (0 if name == "q" else T), T), T)]

    def grad_moves(group, k, sender):
        name = group[0]
        buf, begin = stage(name, k), al(starts(sender) * TILE, TILE)
        if name in "dgu":
            parts = [(PART, MAIN - PART), (MAIN, TILE)] if group in LAST else [PARTS[group]]
            if name == "d":
                return [(buf.at[pl.ds(c, size), :], first["d"].at[pl.ds(al(begin + c, TILE), size), :]) for c, size in parts]
            return [(buf.at[:, pl.ds(c, size)], first[name].at[:, pl.ds(al(begin + c, TILE), size)]) for c, size in parts]
        if name == "o":
            return [(buf, first["o"].at[rows_of(sender), :])]
        if name == "q":
            return [(buf, first["q"].at[:, rows_of(sender)])]
        return [(buf, kv_g.at[k - 1])]

    def grad_send(group, k, act_on):
        for i, (src, dst) in enumerate(grad_moves(group, k, f)):

            def run(i=i, src=src, dst=dst):
                if isinstance(k, int) and k == 0:
                    cp = here(src, dst, e_local[group, i])
                    cp.wait() if act_on == "wait" else cp.start()
                else:
                    cp = remote(src, dst, e_sem[group, i] + k - 1, plane(k))
                    cp.wait_send() if act_on == "wait" else cp.start()

            if i == 0:
                run()
            else:
                pl.when(full(f))(run)

    def grad_take(group):
        for k in (1, 2, 3):
            sender = flip(f, k)
            for i, (src, dst) in enumerate(grad_moves(group, k, sender)):

                def run(i=i, src=src, dst=dst):
                    remote(src, dst, e_sem[group, i] + k - 1, plane(k)).wait_recv()

                if i == 0:
                    run()
                else:
                    pl.when(full(sender))(run)

    def sent(*groups):
        for group in groups:
            for k in (1, 2, 3):
                grad_send(group, k, "wait")

    def block_cols(k):
        return pl.ds(al(flip(f, k) * 512, 512), 512)

    def each_owner(product, *groups):
        @pl.loop(0, 4)
        def _(i):
            k = (i + 1) % 4
            product(k)

            @pl.when(k != 0)
            def _():
                for group in groups:
                    grad_send(group, k, "start")

            @pl.when(k == 0)
            def _():
                for group in groups:
                    if group != "k":
                        grad_send(group, 0, "start")

    def down_grads(group):
        c, size = PARTS[group]

        def product(k):
            stage("d", k)[c : c + size, :] = tn(act[:, c : c + size], ct[:, block_cols(k)]).astype(BF)

        each_owner(product, group)

    def feed_grads(name, which, right):
        c = 0 if which == "A" else PART

        def product(k):
            @pl.loop(0, 2)
            def _(i):
                xs = x2[:, pl.ds(al(flip(f, k) * 512 + i * T, T), T)]
                stage(name, k)[pl.ds(al(i * T, T), T), c : c + PART] = tn(xs, right[:, c : c + PART]).astype(BF)

        each_owner(product, name + which)

    for group in ("dA", "dB", "dC"):
        down_grads(group)

    def feed_back():
        column_each("d", True, lambda cp: cp.wait_recv())

        @pl.loop(0, 4)
        def _(b):
            @pl.loop(0, WIN // UNITS)
            def _(j):
                cols = pl.ds(al(j * UNITS, UNITS), UNITS)
                back = nt(ct[rows_of(b), :], w_d[cols, :])
                dg[rows_of(b), cols] = (back * dg[rows_of(b), cols].astype(F32)).astype(BF)
                du[rows_of(b), cols] = (back * du[rows_of(b), cols].astype(F32)).astype(BF)

    def gate_A():
        gather_drain(1, ct, False, cot_in.at[0, :, half])
        feed_grads("g", "A", dg)

    d2_first, d2_own = scatter_steps(
        lambda b, c: nt(dg[rows_of(b), :], w_g[pl.ds(al(c, COLS), COLS), :]) + nt(du[rows_of(b), :], w_u[pl.ds(al(c, COLS), COLS), :])
    )

    end = (z == 0) | (z == 3)
    middle = (z == 1) | (z == 2)
    next_in = (f, jnp.where(z < 2, 1, 2), t)
    next_out = (f, jnp.where(z < 2, 0, 3), t)
    facing = (f, 3 - z, t)
    across = [next(sems) for _ in range(2 * DEPTH)]
    l_sem = [[next(sems), across[i % (2 * DEPTH)], next(sems)] for i in range(len(CHUNKS))]
    v_sem = [next(local_count) for _ in range(2)]
    o_sem = [next(local_count) for _ in range(4)]

    la, lb, *rest_of_line = (line.at[i] for i in range(8))
    tt, ring = rest_of_line[:2], rest_of_line[2:]

    kept, given = (w_g.at[:, pl.ds(512 + j * TILE, TILE)] for j in range(2))
    even = f % 2 == 0

    def pair_rows(pair, j):
        return pl.ds(j * 512 + pair * T, T)


    def window(arrays, i):
        group, name, r, c, rows, cols = CHUNKS[i]
        if name in "dgu":
            j = flip(r, t) if group in LAST else r
            at = al(starts(j) * TILE + PARTS[group][0], TILE)
            r, c = (at, 0) if name == "d" else (0, at)
        return arrays[name].at[pl.ds(r, rows), pl.ds(c, cols)]

    def line_send(group):
        @pl.when(end)
        def _():
            for i, chunk in enumerate(CHUNKS):
                if chunk[0] == group:
                    remote(window(first, i), window(left, i), l_sem[i][0], next_in).start()

    def add_into(dst, a, b, rows, cols):
        @pl.loop(0, rows // STEP)
        def _(i):
            at = sub(i)
            dst[at, pl.ds(0, cols)] = (a[at, pl.ds(0, cols)].astype(F32) + b[at, pl.ds(0, cols)].astype(F32)).astype(BF)

    def line_one(i):
        _, name, r, c, rows, cols = CHUNKS[i]
        part = (pl.ds(0, rows), pl.ds(0, cols))
        a, b, keep = la.at[part], lb.at[part], ring[i % DEPTH]

        @pl.when(middle)
        def _():
            get_a = here(window(first, i), a, v_sem[0])
            get_a.start()
            remote(window(first, i), window(left, i), l_sem[i][0], next_in).wait_recv()
            get_b = here(window(left, i), b, v_sem[1])
            get_b.start()
            get_a.wait()
            get_b.wait()
            add_into(keep, la, lb, rows, cols)
            remote(keep.at[part], window(cross, i), l_sem[i][1], facing).start()

    def line_two(i):
        _, name, r, c, rows, cols = CHUNKS[i]
        part = (pl.ds(0, rows), pl.ds(0, cols))
        keep, done = ring[i % DEPTH], tt[i % 2]

        @pl.when(middle)
        def _():
            remote(keep.at[part], window(cross, i), l_sem[i][1], facing).wait()
            get = here(window(cross, i), lb.at[part], v_sem[1])
            get.start()
            if i >= 2:
                line_out(i - 2)
            get.wait()
            add_into(done, keep, lb, rows, cols)
            remote(done.at[part], window(total, i), l_sem[i][2], next_out).start()
            here(done.at[part], window(total, i), o_sem[i % 4]).start()

    def line_out(i):
        _, name, r, c, rows, cols = CHUNKS[i]
        done = tt[i % 2].at[pl.ds(0, rows), pl.ds(0, cols)]
        remote(done, window(total, i), l_sem[i][2], next_out).wait_send()
        here(done, window(total, i), o_sem[i % 4]).wait()

    pumped, ready = [0, 0], set()

    def ahead():
        i = pumped[0]
        assert CHUNKS[i][0] in ready and i < pumped[1] + DEPTH
        line_one(i)
        pumped[0] += 1

    def behind():
        i = pumped[1]
        assert i < pumped[0]
        line_two(i)
        pumped[1] += 1

    def grad_ready(group):
        grad_take(group)
        grad_send(group, 0, "wait")
        line_send(group)
        ready.add(group)

    g_sum[...] = jnp.zeros((8, H), F32)
    k_sem = [next(sems) for _ in range(3)]
    q_sem = [[next(sems) for _ in range(3)] for _ in range(2)]
    d_ob, d_qkv = ob, dg
    here_half = (lane // HD) == kv_head
    out_local = here(out_s, out_ref.at[:, half], next(local_count))
    out_remote = remote(out_s, out_ref.at[:, half], next(sems), core)
    in_local = here(d_hid, in_grad_ref.at[:, half], next(local_count))
    in_remote = remote(d_hid, in_grad_ref.at[:, half], next(sems), core)
    kv_copy = here(x2.at[pl.ds(0, 512), pl.ds(T, T)], first["k"], next(local_count))
    whole_move = remote(g_whole.at[:, half], g_whole.at[:, half], next(sems), core)
    gain_move = here(g_whole.at[:, pl.ds(al(f * 512, 512), 512)], gain_ref, next(local_count))

    def norm_two_back():
        lh.wait()
        scatter_wait()

        def rows_back(i, carry):
            rows = scattered(i)
            yo[sub(i), :] = rows
            hat = hid[sub(i), :] * r2s[sub(i), 0:1]
            ss_own[1, sub(i), :] = jnp.broadcast_to(jnp.sum(rows * gain_two * hat, axis=-1, keepdims=True), (STEP, TILE))
            return carry + jnp.sum(rows * hat, axis=0, keepdims=True)

        g_sum[1:2, :] = lax.fori_loop(0, T // STEP, rows_back, jnp.zeros((1, H), F32))
        core_sums(1)

        @pl.loop(0, T // STEP)
        def _(i):
            scale = r2s[sub(i), 0:1]
            hat = hid[sub(i), :] * scale
            mean = (ss_own[1, sub(i), 0:1] + ss_other[1, sub(i), 0:1]) * (1.0 / W)
            rows = out_s[sub(i), :].astype(F32) + scale * (yo[sub(i), :] * gain_two - hat * mean)
            d_hid[sub(i), :] = rows
            dh[pl.ds(al(f * T + i * STEP, STEP), STEP), half] = rows.astype(BF)

        gather_start(3, dh, True)

    def dh_take():
        gather_forward(3, dh)
        for k in range(4):
            gather_take(3, dh, k)

    def out_grads():
        sent("dA", "dB", "dC")

        def product(k):
            stage("o", k)[...] = tn(ob[...], dh[:, block_cols(k)]).astype(BF)

        each_owner(product, "o")

        @pl.loop(0, 4)
        def _(b):
            ob[rows_of(b), :] = nt(dh[rows_of(b), :], w_o[...]).astype(BF)

    def attend_back(pair, i_seq):
        s = 2 * pair + i_seq
        bias_of(s)
        kv, keys, values = kv_of(s)
        keys_t = jnp.transpose(kv)[:HD, :].astype(BF)
        c, sn = turns(s)
        d_key = jnp.zeros((4 * T, TILE), F32)
        d_value = jnp.zeros((4 * T, TILE), F32)
        for i in range(2):
            d_query = []
            for parity in range(2):
                q = only(q_buf[rows_of(s), i * TILE : (i + 1) * TILE], parity)
                do = only(d_ob[rows_of(s), i * TILE : (i + 1) * TILE], parity)
                weights = jnp.exp(nt(keys, q) + bias[...].astype(F32) - lse[s, 2 * i + parity : 2 * i + parity + 1, :])
                d_weights = nt(values, do)
                delta = jnp.sum(weights * d_weights, axis=0, keepdims=True)
                d_scores = (weights * (d_weights - delta)).astype(BF)
                d_value = d_value + nn(weights.astype(BF), do)
                d_key = d_key + nn(d_scores, q)
                d_query.append(nn(keys_t, d_scores))
            d_query = jnp.transpose(jnp.concatenate(d_query, 0)) * 0.125
            d_qkv[rows_of(s), i * TILE : (i + 1) * TILE] = turn(d_query, c, -sn).astype(BF)
        d_key = d_key + pltpu.roll(d_key, HD, 1)
        d_value = d_value + pltpu.roll(d_value, HD, 1)
        keep, give = jnp.where(even, d_key, d_value), jnp.where(even, d_value, d_key)
        mine_here = lane // HD == i_seq
        for j in range(4):
            for place, values in ((kept, keep), (given, give)):
                at = pair_rows(pair, j)
                place[at, :] = jnp.where(mine_here, values[j * T : (j + 1) * T, :], place[at, :].astype(F32)).astype(BF)

    pair_move = remote(given, d_kv_pair, next(sems), plane(1))

    def pair_sum():
        pair_move.wait()

        @pl.loop(0, W // STEP)
        def _(i):
            rows = kept[sub(i), :].astype(F32) + d_kv_pair[sub(i), :].astype(F32)
            kept[sub(i), :] = rows.astype(BF)

            @pl.when(i // (512 // STEP) == z)
            def _():
                d_kv[pl.ds(al(i % (512 // STEP) * STEP, STEP), STEP), :] = rows

        for move in d_kv_moves():
            move.start()

    def d_kv_moves():
        return [remote(kept.at[pl.ds(al(flip(z, k) * 512, 512), 512), :], d_kv_recv.at[k - 1], k_sem[k - 1], column(k)) for k in (1, 2, 3)]

    def up_A():
        sent("gA", "gB")
        feed_grads("u", "A", du)

    def d_kv_take():
        for move in d_kv_moves():
            move.wait()

        for s in range(4):
            c, sn = turns(s)
            rows = pl.ds(s // 2 * T, T)
            whole = d_kv[rows, :]
            for k in range(3):
                whole = whole + d_kv_recv[k, rows, :].astype(F32)
            turned = pltpu.roll(whole, HD, 1)
            whole = jnp.where(low_lane, whole, turned) if s % 2 == 0 else jnp.where(low_lane, turned, whole)
            d_qkv[rows_of(s), 2 * TILE : 3 * TILE] = jnp.where(here_half & even, turn(whole, c, -sn), 0.0).astype(BF)
            d_qkv[rows_of(s), 3 * TILE : 4 * TILE] = jnp.where(here_half & ~even, whole, 0.0).astype(BF)

    def qkv_grads():
        gather_drain(2, x2, True)

        def product(k):
            @pl.loop(0, 2)
            def _(i):
                xs = x1[:, pl.ds(al(flip(f, k) * 512 + i * T, T), T)]
                grads = tn(xs, d_qkv[:, 0:512]).astype(BF)
                stage("q", k)[pl.ds(al(i * T, T), T), :] = grads[:, 0:T]
                stage("k", k)[pl.ds(al(i * T, T), T), :] = grads[:, T:]

        each_owner(product, "q", "k")

    d1_first, d1_own = scatter_steps(lambda b, c: nt(d_qkv[rows_of(b), 0:512], w_qkv[pl.ds(al(c, COLS), COLS), :]))
    out_first, out_own = scatter_steps(lambda b, c: nn(act[rows_of(b), :], w_d[:, pl.ds(al(c, COLS), COLS)]))

    def kv_ready():
        grad_take("k")

        @pl.loop(0, 512 // STEP)
        def _(i):
            rows = x2[sub(i), T : 2 * T].astype(F32)
            for k in (1, 2, 3):
                rows = rows + kv_g[k - 1, sub(i), :].astype(F32)
            x2[sub(i), T : 2 * T] = rows.astype(BF)

        kv_copy.start()
        kv_copy.wait()
        line_send("k")
        ready.add("k")

    def norm_one_back():
        scatter_wait()

        def rows_back(i, carry):
            rows = scattered(i)
            yo[sub(i), :] = rows
            hat = xv[sub(i), half].astype(F32) * r1s[sub(i), 0:1]
            ss_own[2, sub(i), :] = jnp.broadcast_to(jnp.sum(rows * gain_one * hat, axis=-1, keepdims=True), (STEP, TILE))
            return carry + jnp.sum(rows * hat, axis=0, keepdims=True)

        g_sum[0:1, :] = lax.fori_loop(0, T // STEP, rows_back, jnp.zeros((1, H), F32))
        for k in (1, 2, 3):
            pl.semaphore_signal(credit, inc=1, device_id=plane(k), device_id_type=MESH)
        pl.semaphore_signal(credit, inc=1, device_id=core, device_id_type=MESH)
        core_sums(2)
        g_plane[f, :, :] = g_sum[...]
        for k in (1, 2, 3):
            remote(g_sum, g_plane.at[f], q_sem[0][k - 1], plane(k)).start()

        @pl.loop(0, T // STEP)
        def _(i):
            scale = r1s[sub(i), 0:1]
            hat = xv[sub(i), half].astype(F32) * scale
            mean = (ss_own[2, sub(i), 0:1] + ss_other[2, sub(i), 0:1]) * (1.0 / W)
            d_hid[sub(i), :] = d_hid[sub(i), :] + scale * (yo[sub(i), :] * gain_one - hat * mean)

        in_local.start()
        in_remote.start()

    def out_begin():
        pl.semaphore_wait(credit, 4)
        out_first()

    def out_end():
        scatter_wait()

        @pl.loop(0, T // STEP)
        def _(i):
            out_s[sub(i), :] = (hid[sub(i), :] + scattered(i)).astype(BF)

        out_local.start()
        out_remote.start()

    def gains_column():
        for k in (1, 2, 3):
            remote(g_sum, g_plane.at[flip(f, k)], q_sem[0][k - 1], plane(k)).wait_recv()
        g_column[z, :, :] = ((g_plane[0, :, :] + g_plane[1, :, :]) + g_plane[2, :, :]) + g_plane[3, :, :]
        for k in (1, 2, 3):
            remote(g_column.at[z], g_column.at[z], q_sem[1][k - 1], column(k)).start()

    def gains_end():
        for k in (1, 2, 3):
            remote(g_column.at[z], g_column.at[flip(z, k)], q_sem[1][k - 1], column(k)).wait_recv()
        g_whole[:, half] = ((g_column[0, :, :] + g_column[1, :, :]) + g_column[2, :, :]) + g_column[3, :, :]
        whole_move.start()
        whole_move.wait()
        gain_move.start()

    steps = {
        "feed_back": feed_back,
        "gate_A": gate_A,
        "d2_first": d2_first,
        "d2_own": d2_own,
        "gate_B": lambda: feed_grads("g", "B", dg),
        "up_A": up_A,
        "up_B": lambda: feed_grads("u", "B", du),
        "relay": scatter_relay,
        "norm_two_back": norm_two_back,
        "dh_take": dh_take,
        "out_grads": out_grads,
        "pair_send": lambda: pair_move.start(),
        "pair_sum": pair_sum,
        "d_kv_take": d_kv_take,
        "qkv_grads": qkv_grads,
        "d1_first": d1_first,
        "d1_own": d1_own,
        "kv_ready": kv_ready,
        "norm_one_back": norm_one_back,
        "out_first": out_begin,
        "out_own": out_own,
        "out_end": out_end,
        "gains_column": gains_column,
        "gains_end": gains_end,
    }
    for step in ORDER:
        if step == "+":
            ahead()
        elif step == "-":
            behind()
        elif step == 1:
            ahead()
            behind()
        elif step in GROUPS:
            grad_ready(step)
        elif step[:6] == "attend":
            attend_back(int(step[6]) // 2, int(step[6]) % 2)
        else:
            steps[step]()
    while pumped[0] < len(CHUNKS):
        ahead()
        behind()
    while pumped[1] < len(CHUNKS):
        behind()

    @pl.when(middle)
    def _():
        line_out(len(CHUNKS) - 2)
        line_out(len(CHUNKS) - 1)

    @pl.when(end)
    def _():
        for i in range(len(CHUNKS)):
            remote(window(first, i), window(left, i), l_sem[i][0], next_in).wait_send()
            remote(window(total, i), window(total, i), l_sem[i][2], next_in).wait_recv()

    gain_move.wait()
    out_local.wait()
    out_remote.wait()
    in_local.wait()
    in_remote.wait()
    weights_drain()
    column_each("d", False, lambda cp: cp.wait_send())
    column_each("u", False, lambda cp: cp.wait_send())
    column_each("qkv", False, lambda cp: cp.wait_send())
    gather_drain(0, x1, False)
    gather_drain(3, dh, True)
    for k in (1, 2, 3):
        remote(own_gain, own_gain, a_sem[k - 1], plane(k)).wait_send()
        remote(tb.at[f], tb.at[f], t_sem[k - 1], plane(k)).wait_send()
        remote(kv_all.at[z], kv_all.at[z], z_sem[k - 1][0], column(k)).wait_send()
        remote(ids.at[z], ids.at[z], z_sem[k - 1][1], column(k)).wait_send()
        remote(g_sum, g_plane.at[f], q_sem[0][k - 1], plane(k)).wait_send()
        remote(g_column.at[z], g_column.at[z], q_sem[1][k - 1], column(k)).wait_send()
        for name in ("uA", "uB", "o", "q", "k"):
            grad_send(name, k, "wait")
    assert (next(sems), next(local_count)) == (REMOTE_SEMS, LOCAL_SEMS)


REMOTE_SEMS, LOCAL_SEMS = 244, 38


def layer_call(inputs, positions, blocks, cotangent, attn_gain, w_query, w_key, w_value, w_out, mlp_gain, w_gate, w_up, w_down):
    frequency = jnp.exp(jnp.arange(HD // 2, dtype=F32) * (-2.0 * math.log(10000.0) / HD))
    turned = frequency[:, None] * positions.astype(F32)
    table = jnp.concatenate([jnp.cos(turned), jnp.sin(turned), jnp.broadcast_to(blocks.astype(F32), (8, T))], 0)
    gains = jnp.concatenate([attn_gain[None], mlp_gain[None], jnp.zeros((6, 512), BF)], 0).astype(F32)
    shape = jax.ShapeDtypeStruct
    grads = [shape((rows, cols), BF) for _, rows, cols in GRADS]
    any_spec = pl.BlockSpec(memory_space=pl.ANY)
    v = pltpu.VMEM
    results = pl.pallas_call(
        layer_kernel,
        out_shape=[shape((T, W), BF), shape((T, W), F32), shape((8, 512), F32)] + grads * 4,
        in_specs=[any_spec] * 11,
        out_specs=[any_spec] * 27,
        scratch_shapes=[
            v((4 * T, W), BF), v((4 * T, W), BF), v((4 * T, W), BF), v((4 * T, W), BF),
            v((W, 512), BF), v((T, W), BF), v((W, WIN), BF), v((W, WIN), BF), v((WIN, W), BF),
            v((4 * T, WIN), BF), v((4 * T, WIN), BF), v((4 * T, WIN), BF),
            v((4 * T, T), BF), v((4, 4, T, TILE), BF), v((4 * T, T), BF),
            v((4, T, H), BF), v((4, T, H), BF), v((2, T, H), BF), v((2, T, 512), BF), v((T, H), F32), v((T, H), F32), v((T, H), F32), v((T, W), BF),
            v((4, 72, T), F32), v((8, W), F32), v((4, 8, T), F32), v((T, TILE), F32), v((T, TILE), F32),
            v((3, T, TILE), F32), v((3, T, TILE), F32), v((4, 8, T), F32), v((4 * T, T), BF),
            v((4 * WIN, 512), BF), v((3, 512, T), BF), v((8, 512, 512), BF),
            v((512, TILE), F32), v((W, TILE), BF), v((3, 512, TILE), BF),
            v((T, H), BF), v((8, H), F32), v((4, 8, H), F32), v((4, 8, H), F32), v((8, W), F32),
            pltpu.SemaphoreType.DMA((REMOTE_SEMS,)), pltpu.SemaphoreType.DMA((REMOTE_SEMS,)),
            pltpu.SemaphoreType.DMA((LOCAL_SEMS,)), pltpu.SemaphoreType.REGULAR,
        ],
        compiler_params=pltpu.CompilerParams(collective_id=0, has_side_effects=True, vmem_limit_bytes=62 << 20),
    )(inputs, table, gains, cotangent, w_query, w_key, w_value, w_out, w_gate, w_up, w_down)
    return finish(*results[:3], *results[-6:])


def finish_kernel(*refs):
    output, input_grad, gains, down, gate, up, out, query, kv = refs[:9]
    targets = refs[9:]
    for source, target in zip((output, input_grad), targets):
        target[0] = source[...]
    attn_target, q_target, k_target, v_target, o_target, mlp_target, g_target, u_target, d_target = targets[2:]
    attn_target[...] = gains[0:1, :]
    mlp_target[...] = gains[1:2, :]
    k_target[...] = kv[:, :TILE].astype(F32)
    v_target[...] = kv[:, TILE:].astype(F32)
    for source, target in ((query, q_target), (out, o_target), (gate, g_target), (up, u_target), (down, d_target)):
        target[...] = source[...].astype(F32)


def finish(output, input_grad, gains, down, gate, up, out, query, kv):
    parts = 4
    shape = jax.ShapeDtypeStruct

    def rows(count, cols):
        return pl.BlockSpec((count // parts, cols), lambda i: (i, 0))

    def page(count, cols):
        return pl.BlockSpec((1, count // parts, cols), lambda i: (0, i, 0))

    line = pl.BlockSpec((1, 512), lambda i: (0, 0))
    results = pl.pallas_call(
        finish_kernel,
        grid=(parts,),
        in_specs=[rows(T, W), rows(T, W), pl.BlockSpec((8, 512), lambda i: (0, 0))] + [rows(*a.shape) for a in (down, gate, up, out, query, kv)],
        out_specs=[page(T, W), page(T, W), line, rows(512, 1024), rows(512, TILE), rows(512, TILE), rows(1024, 512), line, rows(512, 2816), rows(512, 2816), rows(2816, 512)],
        out_shape=[shape((1, T, W), BF), shape((1, T, W), F32), shape((1, 512), F32)]
        + [shape(a, F32) for a in ((512, 1024), (512, TILE), (512, TILE), (1024, 512), (1, 512), (512, 2816), (512, 2816), (2816, 512))],
        compiler_params=pltpu.CompilerParams(dimension_semantics=("arbitrary",)),
    )(output, input_grad, gains, down, gate, up, out, query, kv)
    results = list(results)
    results[2], results[7] = results[2][0], results[7][0]
    return tuple(results)


def solution(mesh):
    n, m = mesh.shape["fsdp"], mesh.shape["ctx"]

    def step(*args):
        return layer_call(*args) if n == m == 4 else local(n, m, *args)

    return jax.shard_map(
        step,
        mesh=mesh,
        in_specs=(
            P("fsdp", "ctx", None),
            P("fsdp", "ctx"),
            P("fsdp", "ctx"),
            P("fsdp", "ctx", None),
            P("fsdp"),
            P("fsdp", "tp"),
            P("fsdp", "tp"),
            P("fsdp", "tp"),
            P("tp", "fsdp"),
            P("fsdp"),
            P("fsdp", "tp"),
            P("fsdp", "tp"),
            P("tp", "fsdp"),
        ),
        out_specs=(
            P("fsdp", "ctx", None),
            P("fsdp", "ctx", None),
            P("fsdp"),
            P("fsdp", "tp"),
            P("fsdp", "tp"),
            P("fsdp", "tp"),
            P("tp", "fsdp"),
            P("fsdp"),
            P("fsdp", "tp"),
            P("fsdp", "tp"),
            P("tp", "fsdp"),
        ),
        check_vma=False,
    )
```

profile of v0, /device:TPU:0, one launch (start us, length us, event | category | flops | bytes accessed | tf_op | source)
XLA Modules:
  0.0 480.3 jit_solution(15586559507768038027)
XLA Ops:
  0.7 0.1 pad.2.clone
  0.7 0.7 convert_element_type.9
  1.4 0.7 convert_element_type.10
  2.1 0.7 broadcast_in_dim.19
  2.8 0.7 broadcast_in_dim.20
  3.5 0.7 maximum_convert_fusion.refs_2_
  4.1 0.2 multiply_cosine_fusion
  4.3 0.6 pad_maximum_fusion.refs_1_
  5.0 461.4 %shard_map.212 = (bf16[256,2048]{1,0:T(8,128)(2,1)}, f32[256,2048]{1,0:T(8,128)}, f32[8,512]{1,0:T(8,128)}, bf16[2816,512]{1,0:T(8,128)(2,1)}, bf16[512,2816]{1,...) custom-call(bf16[1,256,2048]{2,1,0:T(8,128)(2,1)} %refs_0_.1, ...), custom_call_target="tpu_custom_call" | custom-call | tf_op jit(solution)/shard_map/pallas_call | solution.py:1315
  466.4 13.7 %shard_map.213 = (bf16[1,256,2048]{2,1,0:T(8,128)(2,1)}, f32[1,256,2048]{2,1,0:T(8,128)}, f32[1,512]{1,0:T(1,128)}, f32[512,1024]{1,0:T(8,128)}, f32[512,128]{1,...) custom-call(bf16[256,2048]{1,0:T(8,128)(2,1)} %get-tuple-element.31., ...), custom_call_target="tpu_custom_call" | custom-call | tf_op jit(solution)/shard_map/pallas_call | solution.py:1364
  (3 shorter events, 0.0 us)
where the time goes:
time: 483 us; the launch traced here: 480 us
  Pallas kernels  475 us (98%)
    pallas_call x1, Pallas kernels, layer_call(): pl.pallas_call(layer_kernel, out_shape=[shape((T, W), BF), shape((T, W),...  461 us
    pallas_call x1, Pallas kernels, finish(): pl.pallas_call(finish_kernel, grid=(parts,), in_specs=[rows(T, W), rows(T...  13.7 us

commit v1 on v0

--- a/solution.py
+++ b/solution.py
@@ -264,8 +264,8 @@
 CHUNKS = chunk_list()
 DEPTH = 4
 ORDER = (
-    "dA", "+", "feed_back", 1, 1, 1, "dB", "gate_A", 1, 1, "d2_first", 1, "d2_own", 1, "dC", "relay", 1, 1, "gate_B", "gA", 1,
-    "norm_two_back", 1, 1, 1, "gB", "up_A", 1, 1, "dh_take", "+", "out_grads", 1, "attend0", 1, "attend1", 1, "uA", "+", "up_B", 1, "attend2", 1,
+    "dA", "+", "feed_back", 1, 1, 1, "dB", 1, "gate_A", 1, 1, "d2_first", 1, "d2_own", "dC", 1, "relay", 1, "gate_B", "gA", 1, 1, 1,
+    "norm_two_back", 1, "gB", "up_A", 1, 1, "dh_take", "+", "out_grads", 1, "attend0", 1, "attend1", 1, "uA", "+", "up_B", 1, "attend2", 1,
     "attend3", "pair_send", 1, "-", "pair_sum", "uB", "+", 1, "o", "d_kv_take", 1, "qkv_grads", 1, "d1_first", 1, "d1_own", 1, "q", 1, "relay", 1,
     "kv_ready", 1, 1, "norm_one_back", 1, "out_first", 1, "out_own", 1, "relay", 1, "-", "gains_column", "-", "out_end", "gains_end",
 )
@@ -294,12 +294,12 @@
     def take(count):
         return [next(names) for _ in range(count)]
 
-    x_in, table_in, gains_in, cot_in, wq, wk, wv, wo, wg, wu, wd = take(11)
+    x_in, place_in, block_in, gain_in_one, gain_in_two, cot_in, wq, wk, wv, wo, wg, wu, wd = take(13)
     out_ref, in_grad_ref, gain_ref = take(3)
     first, left, cross, total = ({name: next(names) for name, _, _ in GRADS} for _ in range(4))
     (x1, x2, ct, dh, w_qkv, w_o, w_g, w_u, w_d, act, dg, du, q_buf, kv_all, ob) = take(15)
     (ps, pr, rr, rd, yo, hid, d_hid, xv, tb, ga, ids, r1s, r2s, ss_own, ss_other, lse, bias) = take(17)
-    (gs_d, kv_g, line, d_kv, d_kv_pair, d_kv_recv, out_s, g_sum, g_plane, g_column, g_whole) = take(11)
+    (gs_d, line, waves, d_kv, d_kv_recv, out_s, g_sum, g_plane, g_column, g_whole) = take(10)
     send_sem, recv_sem, local_sem, credit = take(4)
     f, z, t = lax.axis_index("fsdp"), lax.axis_index("ctx"), lax.axis_index("tp")
     sems = iter(range(10**6))
@@ -336,10 +336,11 @@
     lc.start()
     lh = here(cot_in.at[0, :, half], out_s, next(local_count))
     lh.start()
-    lt = here(table_in, tb.at[f], next(local_count))
-    lt.start()
-    lg = here(gains_in, ga.at[:, pl.ds(al(f * 512, 512), 512)], next(local_count))
-    lg.start()
+    own_gain = ga.at[:, pl.ds(al(f * 512, 512), 512)]
+    own_gain[0:1, :] = gain_in_one[...].astype(F32).reshape(1, 512)
+    own_gain[1:2, :] = gain_in_two[...].astype(F32).reshape(1, 512)
+    tb[f, 0:1, :] = place_in[...].astype(F32)
+    tb[f, 1:2, :] = block_in[...].astype(F32)
 
     def starts(r):
         return (11 * r + 1 - t) // 2
@@ -497,8 +498,6 @@
 
     t_sem = [next(sems) for _ in range(3)]
     a_sem = [next(sems) for _ in range(3)]
-    own_gain = ga.at[:, pl.ds(al(f * 512, 512), 512)]
-
     barrier = pltpu.get_barrier_semaphore()
     for k in (1, 2, 3):
         pl.semaphore_signal(barrier, inc=1, device_id=plane(k), device_id_type=MESH)
@@ -506,8 +505,6 @@
     pl.semaphore_signal(barrier, inc=1, device_id=core, device_id_type=MESH)
     pl.semaphore_wait(barrier, 7)
 
-    lt.wait()
-    lg.wait()
     for k in (1, 2, 3):
         remote(own_gain, own_gain, a_sem[k - 1], plane(k)).start()
         remote(tb.at[f], tb.at[f], t_sem[k - 1], plane(k)).start()
@@ -556,12 +553,15 @@
     first_half = lane % HD < HD // 2
     kv_head = f // 2
 
+    def make_turns(b):
+        exponent = lax.broadcasted_iota(jnp.int32, (HD // 2, T), 0).astype(F32) * (-2.0 * math.log(10000.0) / HD)
+        turned = jnp.exp(exponent) * tb[b, 0:1, :]
+        cosine, sine = jnp.cos(turned), jnp.sin(turned)
+        waves[b, 0, :, :] = jnp.transpose(jnp.concatenate([cosine] * 4, 0))
+        waves[b, 1, :, :] = jnp.transpose(jnp.concatenate([-sine, sine, -sine, sine], 0))
+
     def turns(b):
-        cosine, sine = tb[b, 0:32, :], tb[b, 32:64, :]
-        return (
-            jnp.transpose(jnp.concatenate([cosine] * 4, 0)),
-            jnp.transpose(jnp.concatenate([-sine, sine, -sine, sine], 0)),
-        )
+        return waves[b, 0, :, :], waves[b, 1, :, :]
 
     def turn(v, c, s):
         swapped = jnp.where(first_half, pltpu.roll(v, TILE - 32, 1), pltpu.roll(v, 32, 1))
@@ -570,6 +570,7 @@
     def qkv_block(k):
         b = flip(f, k)
         qkv = nn(x1[rows_of(b), :], w_qkv[...])
+        make_turns(b)
         c, s = turns(b)
         for i in range(2):
             q = turn(qkv[:, i * TILE : (i + 1) * TILE], c, s) * 0.125
@@ -579,7 +580,7 @@
         key = jnp.where(kv_head == 0, key, pltpu.roll(key, HD, 1))
         value = jnp.where(kv_head == 1, value, pltpu.roll(value, HD, 1))
         kv_all[z, b, :, :] = jnp.where(low_lane, key, value).astype(BF)
-        ids[z, pl.ds(b, 1), :] = tb[b, 64:65, :]
+        ids[z, pl.ds(b, 1), :] = tb[b, 1:2, :]
 
     qkv_block(0)
     for k in (1, 2, 3):
@@ -785,6 +786,9 @@
 
     e_sem = {(name, i): [next(sems) for _ in range(3)][0] for name in GROUPS for i in range(2 if name in LAST else 1)}
     e_local = {(name, i): next(local_count) for name in GROUPS for i in range(2 if name in LAST else 1)}
+
+    def kv_place(k):
+        return w_u.at[pl.ds(al((k - 1) * 512, 512), 512), pl.ds(0, T)]
 
     def stage(name, k):
         if name == "d":
@@ -807,7 +811,7 @@
             return [(buf, first["o"].at[rows_of(sender), :])]
         if name == "q":
             return [(buf, first["q"].at[:, rows_of(sender)])]
-        return [(buf, kv_g.at[k - 1])]
+        return [(buf, kv_place(k))]
 
     def grad_send(group, k, act_on):
         for i, (src, dst) in enumerate(grad_moves(group, k, f)):
@@ -1042,6 +1046,7 @@
             d_hid[sub(i), :] = rows
             dh[pl.ds(al(f * T + i * STEP, STEP), STEP), half] = rows.astype(BF)
 
+        column_each("u", False, lambda cp: cp.wait_send())
         gather_start(3, dh, True)
 
     def dh_take():
@@ -1092,6 +1097,7 @@
                 at = pair_rows(pair, j)
                 place[at, :] = jnp.where(mine_here, values[j * T : (j + 1) * T, :], place[at, :].astype(F32)).astype(BF)
 
+    d_kv_pair = w_u.at[:, pl.ds(T, TILE)]
     pair_move = remote(given, d_kv_pair, next(sems), plane(1))
 
     def pair_sum():
@@ -1154,7 +1160,7 @@
         def _(i):
             rows = x2[sub(i), T : 2 * T].astype(F32)
             for k in (1, 2, 3):
-                rows = rows + kv_g[k - 1, sub(i), :].astype(F32)
+                rows = rows + kv_place(k)[sub(i), :].astype(F32)
             x2[sub(i), T : 2 * T] = rows.astype(BF)
 
         kv_copy.start()
@@ -1284,7 +1290,6 @@
     in_remote.wait()
     weights_drain()
     column_each("d", False, lambda cp: cp.wait_send())
-    column_each("u", False, lambda cp: cp.wait_send())
     column_each("qkv", False, lambda cp: cp.wait_send())
     gather_drain(0, x1, False)
     gather_drain(3, dh, True)
@@ -1300,14 +1305,10 @@
     assert (next(sems), next(local_count)) == (REMOTE_SEMS, LOCAL_SEMS)
 
 
-REMOTE_SEMS, LOCAL_SEMS = 244, 38
+REMOTE_SEMS, LOCAL_SEMS = 244, 36
 
 
 def layer_call(inputs, positions, blocks, cotangent, attn_gain, w_query, w_key, w_value, w_out, mlp_gain, w_gate, w_up, w_down):
-    frequency = jnp.exp(jnp.arange(HD // 2, dtype=F32) * (-2.0 * math.log(10000.0) / HD))
-    turned = frequency[:, None] * positions.astype(F32)
-    table = jnp.concatenate([jnp.cos(turned), jnp.sin(turned), jnp.broadcast_to(blocks.astype(F32), (8, T))], 0)
-    gains = jnp.concatenate([attn_gain[None], mlp_gain[None], jnp.zeros((6, 512), BF)], 0).astype(F32)
     shape = jax.ShapeDtypeStruct
     grads = [shape((rows, cols), BF) for _, rows, cols in GRADS]
     any_spec = pl.BlockSpec(memory_space=pl.ANY)
@@ -1315,7 +1316,7 @@
     results = pl.pallas_call(
         layer_kernel,
         out_shape=[shape((T, W), BF), shape((T, W), F32), shape((8, 512), F32)] + grads * 4,
-        in_specs=[any_spec] * 11,
+        in_specs=[any_spec] + [pl.BlockSpec(memory_space=pltpu.VMEM)] * 4 + [any_spec] * 8,
         out_specs=[any_spec] * 27,
         scratch_shapes=[
             v((4 * T, W), BF), v((4 * T, W), BF), v((4 * T, W), BF), v((4 * T, W), BF),
@@ -1323,16 +1324,16 @@
             v((4 * T, WIN), BF), v((4 * T, WIN), BF), v((4 * T, WIN), BF),
             v((4 * T, T), BF), v((4, 4, T, TILE), BF), v((4 * T, T), BF),
             v((4, T, H), BF), v((4, T, H), BF), v((2, T, H), BF), v((2, T, 512), BF), v((T, H), F32), v((T, H), F32), v((T, H), F32), v((T, W), BF),
-            v((4, 72, T), F32), v((8, W), F32), v((4, 8, T), F32), v((T, TILE), F32), v((T, TILE), F32),
+            v((4, 8, T), F32), v((8, W), F32), v((4, 8, T), F32), v((T, TILE), F32), v((T, TILE), F32),
             v((3, T, TILE), F32), v((3, T, TILE), F32), v((4, 8, T), F32), v((4 * T, T), BF),
-            v((4 * WIN, 512), BF), v((3, 512, T), BF), v((8, 512, 512), BF),
-            v((512, TILE), F32), v((W, TILE), BF), v((3, 512, TILE), BF),
+            v((4 * WIN, 512), BF), v((8, 512, 512), BF), v((4, 2, T, TILE), F32),
+            v((512, TILE), F32), v((3, 512, TILE), BF),
             v((T, H), BF), v((8, H), F32), v((4, 8, H), F32), v((4, 8, H), F32), v((8, W), F32),
             pltpu.SemaphoreType.DMA((REMOTE_SEMS,)), pltpu.SemaphoreType.DMA((REMOTE_SEMS,)),
             pltpu.SemaphoreType.DMA((LOCAL_SEMS,)), pltpu.SemaphoreType.REGULAR,
         ],
         compiler_params=pltpu.CompilerParams(collective_id=0, has_side_effects=True, vmem_limit_bytes=62 << 20),
-    )(inputs, table, gains, cotangent, w_query, w_key, w_value, w_out, w_gate, w_up, w_down)
+    )(inputs, positions, blocks, attn_gain, mlp_gain, cotangent, w_query, w_key, w_value, w_out, w_gate, w_up, w_down)
     return finish(*results[:3], *results[-6:])
 
 

time: 483 us -> 475 us (0.983)
  no operation moved by 1% of the time
where the time goes in v1:
time: 475 us; the launch traced here: 472 us
  Pallas kernels  471 us (99%)
    pallas_call x1, Pallas kernels, layer_call(): pl.pallas_call(layer_kernel, out_shape=[shape((T, W), BF), shape((T, W),...  457 us
    pallas_call x1, Pallas kernels, finish(): pl.pallas_call(finish_kernel, grid=(parts,), in_specs=[rows(T, W), rows(T...  13.9 us

profile of v1, /device:TPU:0, one launch (start us, length us, event | category | flops | bytes accessed | tf_op | source)
XLA Modules:
  0.0 472.1 jit_solution(12465982110569392024)
XLA Ops:
  0.6 457.4 %shard_map.212 = (bf16[256,2048]{1,0:T(8,128)(2,1)}, f32[256,2048]{1,0:T(8,128)}, f32[8,512]{1,0:T(8,128)}, bf16[2816,512]{1,0:T(8,128)(2,1)}, bf16[512,2816]{1,...) custom-call(bf16[1,256,2048]{2,1,0:T(8,128)(2,1)} %refs_0_.1, ...), custom_call_target="tpu_custom_call" | custom-call | tf_op jit(solution)/shard_map/pallas_call | solution.py:1316
  458.1 13.9 %shard_map.213 = (bf16[1,256,2048]{2,1,0:T(8,128)(2,1)}, f32[1,256,2048]{2,1,0:T(8,128)}, f32[1,512]{1,0:T(1,128)}, f32[512,1024]{1,0:T(8,128)}, f32[512,128]{1,...) custom-call(bf16[256,2048]{1,0:T(8,128)(2,1)} %get-tuple-element.31., ...), custom_call_target="tpu_custom_call" | custom-call | tf_op jit(solution)/shard_map/pallas_call | solution.py:1365

commit v2 on v1

--- a/solution.py
+++ b/solution.py
@@ -915,7 +915,7 @@
     next_out = (f, jnp.where(z < 2, 0, 3), t)
     facing = (f, 3 - z, t)
     across = [next(sems) for _ in range(2 * DEPTH)]
-    l_sem = [[next(sems), across[i % (2 * DEPTH)], next(sems)] for i in range(len(CHUNKS))]
+    l_sem = [[s, across[i % (2 * DEPTH)], s] for i, s in enumerate([next(sems) for _ in CHUNKS])]
     v_sem = [next(local_count) for _ in range(2)]
     o_sem = [next(local_count) for _ in range(4)]
 
@@ -1305,7 +1305,7 @@
     assert (next(sems), next(local_count)) == (REMOTE_SEMS, LOCAL_SEMS)
 
 
-REMOTE_SEMS, LOCAL_SEMS = 244, 36
+REMOTE_SEMS, LOCAL_SEMS = 206, 36
 
 
 def layer_call(inputs, positions, blocks, cotangent, attn_gain, w_query, w_key, w_value, w_out, mlp_gain, w_gate, w_up, w_down):
@@ -1352,7 +1352,7 @@
 
 
 def finish(output, input_grad, gains, down, gate, up, out, query, kv):
-    parts = 4
+    parts = 2
     shape = jax.ShapeDtypeStruct
 
     def rows(count, cols):

time: 475 us -> 473 us (level)
  no operation moved by 1% of the time
where the time goes in v2:
time: 473 us; the launch traced here: 471 us
  Pallas kernels  470 us (99%)
    pallas_call x1, Pallas kernels, layer_call(): pl.pallas_call(layer_kernel, out_shape=[shape((T, W), BF), shape((T, W),...  457 us
    pallas_call x1, Pallas kernels, finish(): pl.pallas_call(finish_kernel, grid=(parts,), in_specs=[rows(T, W), rows(T...  13 us

profile of v2, /device:TPU:0, one launch (start us, length us, event | category | flops | bytes accessed | tf_op | source)
XLA Modules:
  0.0 470.6 jit_solution(17483628177647379494)
XLA Ops:
  0.6 456.8 %shard_map.212 = (bf16[256,2048]{1,0:T(8,128)(2,1)}, f32[256,2048]{1,0:T(8,128)}, f32[8,512]{1,0:T(8,128)}, bf16[2816,512]{1,0:T(8,128)(2,1)}, bf16[512,2816]{1,...) custom-call(bf16[1,256,2048]{2,1,0:T(8,128)(2,1)} %refs_0_.1, ...), custom_call_target="tpu_custom_call" | custom-call | tf_op jit(solution)/shard_map/pallas_call | solution.py:1316
  457.4 13.0 %shard_map.213 = (bf16[1,256,2048]{2,1,0:T(8,128)(2,1)}, f32[1,256,2048]{2,1,0:T(8,128)}, f32[1,512]{1,0:T(1,128)}, f32[512,1024]{1,0:T(8,128)}, f32[512,128]{1,...) custom-call(bf16[256,2048]{1,0:T(8,128)(2,1)} %get-tuple-element.31., ...), custom_call_target="tpu_custom_call" | custom-call | tf_op jit(solution)/shard_map/pallas_call | solution.py:1365
